TPU v7x, 32 devices: a whole 2x2x4 slice. The times are simulated.
32 devices in a mesh: groups: 2 (over y), rows: 16 (over z, x, core), cols: 1.
Axes of the slice: x: 2, y: 2, z: 4, core: 2. Of those that a mesh axis runs over, the one named last changes fastest.
Arguments:
- pair_in: bfloat16 [256, 128, 128], P(('groups', 'rows'), 'cols'), parts along dimension 0, may hold values from -6 to 450
- single_in: float32 [256, 384], P(('groups', 'rows')), parts along dimension 0, may hold values from -6 to 6
- frames_in: float32 [12, 256], P(None, ('groups', 'rows')), parts along dimension 1, may hold values from -3 to 3, as said below
- dist_bins: int32 [2, 256, 128], P(None, ('groups', 'rows'), 'cols'), parts along dimension 1, may hold values from 0 to 14
- res_mask: int32 [256], P('groups'), parts along dimension 0, may hold values from 0 to 1, as said below
- chain_ids: int32 [256], P('groups'), parts along dimension 0, may hold values from 0 to 7, never falling along the last dimension, each value on 1 to 32 neighbouring positions
- w_left: bfloat16 [384, 128], replicated, may hold values from -0.3125 to 0.3125
- w_right: bfloat16 [384, 128], replicated, may hold values from -0.3125 to 0.3125
- dist_embed: bfloat16 [15, 128], replicated, may hold values from -6 to 6
- chain_embed: bfloat16 [2, 128], replicated, may hold values from -6 to 6
- pair_gain: float32 [128], replicated, may hold values from 0.5 to 1.5
- mlp_in: bfloat16 [128, 512], replicated, may hold values from -0.5 to 0.5
- mlp_bias: float32 [512], replicated, may hold values from -3 to 3
- mlp_out: bfloat16 [512, 128], replicated, may hold values from -0.25 to 0.25
- w_qkv: bfloat16 [384, 576], replicated, may hold values from -0.3125 to 0.3125
- w_points: bfloat16 [384, 576], replicated, may hold values from -0.3125 to 0.3125
- bias_weight: bfloat16 [128, 12], replicated, may hold values from -0.5 to 0.5
- point_scale: float32 [12], replicated, may hold values from 0.3 to 3
- w_out: bfloat16 [2112, 384], replicated, may hold values from -0.125 to 0.125
- single_gain: float32 [384], replicated, may hold values from 0.5 to 1.5
- w_frame: bfloat16 [384, 6], replicated, may hold values from -0.3125 to 0.3125
Outputs:
- pair_out: bfloat16 [256, 128, 128], P(('groups', 'rows'), 'cols'), parts along dimension 0
- single_out: float32 [256, 384], P(('groups', 'rows')), parts along dimension 0
- frames_out: float32 [12, 256], P(None, ('groups', 'rows')), parts along dimension 1
There are 2 independent parts, one for each index of `groups`. A program takes and returns all parts, laid end to end along the dimension named above; an argument that names none is the same for every part. Nothing has to cross between parts.
Inputs may be any that keep to these rules, and one draw needn't show every extreme that they name: `frames_in`: column n holds a rotation matrix in rows 0 to 8 (row-major) and a translation in rows 9 to 11. `res_mask`: 1 on a prefix of the residues, at least 64 and at most 127 of them. `chain_ids`: never falling along the residues; a chain holds 1 to 32 residues.
All inputs are finite; a program needn't handle non-finite values.
Results may differ from a plain program's by a relative error of at most 0.022.
Values may be sent and summed in bfloat16 or wider, within the bound.
A program may use at most 64 MiB of HBM per device.

v0:
```python
import math
import jax
import jax.numpy as jnp
from jax import lax
from jax.sharding import PartitionSpec as P

NQP = 4
CYCLES = 2
HIGHEST = lax.Precision.HIGHEST


def layer_norm(values, norm_gain):
    centre = jnp.mean(values, axis=-1, keepdims=True)
    spread = values - centre
    second = jnp.mean(spread * spread, axis=-1, keepdims=True)
    return spread * lax.rsqrt(second + 1e-05) * norm_gain


def to_global(points, frames):
    turns = frames[:, :9].reshape(-1, 3, 3)
    return jnp.einsum("nab,nbx->nax", turns, points, precision=HIGHEST) + frames[:, 9:12, None]


def to_local(points, frames):
    turns = frames[:, :9].reshape(-1, 3, 3)
    return jnp.einsum("nab,nax->nbx", turns, points - frames[:, 9:12, None], precision=HIGHEST)


def update_frames(frames, frame_step):
    quat_scale = lax.rsqrt(1.0 + jnp.sum(frame_step[:, :3] * frame_step[:, :3], axis=1))
    quat_b = frame_step[:, 0] * quat_scale
    quat_c = frame_step[:, 1] * quat_scale
    quat_d = frame_step[:, 2] * quat_scale
    entries = [
        quat_scale * quat_scale + quat_b * quat_b - quat_c * quat_c - quat_d * quat_d,
        2.0 * (quat_b * quat_c - quat_scale * quat_d),
        2.0 * (quat_b * quat_d + quat_scale * quat_c),
        2.0 * (quat_b * quat_c + quat_scale * quat_d),
        quat_scale * quat_scale - quat_b * quat_b + quat_c * quat_c - quat_d * quat_d,
        2.0 * (quat_c * quat_d - quat_scale * quat_b),
        2.0 * (quat_b * quat_d - quat_scale * quat_c),
        2.0 * (quat_c * quat_d + quat_scale * quat_b),
        quat_scale * quat_scale - quat_b * quat_b - quat_c * quat_c + quat_d * quat_d,
    ]
    turn_matrix = jnp.stack(entries, axis=1).reshape(-1, 3, 3)
    before = frames[:, :9].reshape(-1, 3, 3)
    rotated = jnp.einsum("nab,nbc->nac", before, turn_matrix, precision=HIGHEST)
    new_shift = (
        jnp.einsum("nab,nb->na", before, frame_step[:, 3:6], precision=HIGHEST) + frames[:, 9:12]
    )
    return jnp.concatenate([rotated.reshape(-1, 9), new_shift], axis=1)


def update_row(
    pair_row,
    bins_row,
    left_row,
    mask_row,
    same_row,
    right_keys,
    dist_embed,
    chain_embed,
    pair_gain,
    mlp_in,
    mlp_bias,
    mlp_out,
):
    onehot = (
        bins_row[:, None] == jnp.arange(dist_embed.shape[0], dtype=jnp.int32)[None, :]
    ).astype(jnp.bfloat16)
    looked = jnp.dot(onehot, dist_embed, preferred_element_type=jnp.float32)
    chain_part = jnp.where(
        same_row[:, None], chain_embed[1].astype(jnp.float32), chain_embed[0].astype(jnp.float32)
    )
    summed = (
        pair_row.astype(jnp.float32)
        + mask_row[:, None] * (left_row[None, :] + right_keys.astype(jnp.float32))
        + looked
        + chain_part
    )
    normed = layer_norm(summed, pair_gain).astype(jnp.bfloat16)
    hidden = jax.nn.relu(
        jnp.dot(normed, mlp_in, preferred_element_type=jnp.float32) + mlp_bias
    ).astype(jnp.bfloat16)
    mixed_out = jnp.dot(hidden, mlp_out, preferred_element_type=jnp.float32)
    return (summed + mask_row[:, None] * mixed_out).astype(jnp.bfloat16)


def attention_logits(
    queries, query_points, key_heads, key_points, pair_tile, key_live, bias_weight, point_scale
):
    head_dim = queries.shape[2]
    scores = jnp.einsum(
        "ihd,jhd->ihj", queries, key_heads, preferred_element_type=jnp.float32
    ) * head_dim ** (-0.5)
    biases = jnp.einsum("ijc,ch->ihj", pair_tile, bias_weight, preferred_element_type=jnp.float32)
    query_sq = jnp.sum(query_points * query_points, axis=(1, 3))
    key_sq = jnp.sum(key_points * key_points, axis=(1, 3))
    cross_term = jnp.einsum("iahp,jahp->ihj", query_points, key_points, precision=HIGHEST)
    distance = query_sq[:, :, None] + key_sq.T[None, :, :] - 2.0 * cross_term
    point_weight = math.sqrt(2.0 / (9.0 * query_points.shape[3])) / 2.0
    logits = math.sqrt(1.0 / 3.0) * (
        scores + biases - point_scale[None, :, None] * point_weight * distance
    )
    return jnp.where(key_live[None, None, :], logits, -1e30)


def build_features(row_total, attended, point_sum, pair_sum, frames_rows):
    row_count = row_total.shape[0]
    attended = attended / row_total[:, :, None]
    point_sum = point_sum / row_total[:, None, :, None]
    pair_sum = pair_sum / row_total[:, :, None]
    local_points = to_local(point_sum.reshape(row_count, 3, -1), frames_rows).reshape(
        point_sum.shape
    )
    lengths = jnp.sqrt(jnp.sum(local_points * local_points, axis=1) + 1.0)
    return jnp.concatenate(
        [
            attended.reshape(row_count, -1),
            local_points.reshape(row_count, -1),
            lengths.reshape(row_count, -1),
            pair_sum.reshape(row_count, -1),
        ],
        axis=1,
    ).astype(jnp.bfloat16)


def finish_rows(
    single_rows,
    frames_rows,
    row_total,
    attended,
    point_sum,
    pair_sum,
    head_count,
    head_dim,
    value_count,
    channels,
    w_out,
    single_gain,
    w_frame,
):
    rows_here = single_rows.shape[0]
    features = build_features(
        row_total,
        attended.reshape(rows_here, head_count, head_dim),
        point_sum.reshape(rows_here, 3, head_count, value_count),
        pair_sum.reshape(rows_here, head_count, channels),
        frames_rows,
    )
    update = jnp.dot(features, w_out, preferred_element_type=jnp.float32)
    single_rows = layer_norm(single_rows + update, single_gain)
    frame_step = jnp.dot(
        single_rows.astype(jnp.bfloat16), w_frame, preferred_element_type=jnp.float32
    )
    return (single_rows, update_frames(frames_rows, frame_step))


def shards(
    pair_in,
    single_in,
    frames_in,
    dist_bins,
    res_mask,
    chain_ids,
    w_left,
    w_right,
    dist_embed,
    chain_embed,
    pair_gain,
    mlp_in,
    mlp_bias,
    mlp_out,
    w_qkv,
    w_points,
    bias_weight,
    point_scale,
    w_out,
    single_gain,
    w_frame,
):
    row_count = pair_in.shape[0]
    key_count = pair_in.shape[1]
    channels = pair_in.shape[2]
    head_count = bias_weight.shape[1]
    head_dim = w_qkv.shape[1] // (3 * head_count)
    point_count = w_points.shape[1] // (3 * head_count)
    value_count = point_count - 2 * NQP
    row_start = lax.axis_index("rows") * row_count
    key_start = lax.axis_index("cols") * key_count
    row_live = lax.dynamic_slice_in_dim(res_mask, row_start, row_count).astype(jnp.float32)
    key_mask_int = lax.dynamic_slice_in_dim(res_mask, key_start, key_count)
    key_live = key_mask_int > 0
    pair_mask = row_live[:, None] * key_mask_int.astype(jnp.float32)[None, :]
    same_chain = (
        lax.dynamic_slice_in_dim(chain_ids, row_start, row_count)[:, None]
        == lax.dynamic_slice_in_dim(chain_ids, key_start, key_count)[None, :]
    )
    pair_tile = pair_in
    single = single_in
    frames = frames_in.T
    for cycle_index in range(CYCLES):
        single_bf = single.astype(jnp.bfloat16)
        left_proj = jnp.dot(single_bf, w_left, preferred_element_type=jnp.float32)
        triple = (
            jnp.dot(single_bf, w_qkv, preferred_element_type=jnp.float32)
            .astype(jnp.bfloat16)
            .reshape(row_count, 3, head_count, head_dim)
        )
        own_points = to_global(
            jnp.dot(single_bf, w_points, preferred_element_type=jnp.float32).reshape(
                row_count, 3, head_count * point_count
            ),
            frames,
        ).reshape(row_count, 3, head_count, point_count)
        own_right = jnp.dot(single_bf, w_right, preferred_element_type=jnp.float32).astype(
            jnp.bfloat16
        )
        own_pairs = triple[:, 1:].reshape(row_count, -1)
        own_geometry = own_points[:, :, :, NQP:].reshape(row_count, -1)
        all_right, all_pairs = (
            lax.all_gather(own_right, "rows", axis=0, tiled=True),
            lax.all_gather(own_pairs, "rows", axis=0, tiled=True),
        )
        all_geometry = lax.all_gather(own_geometry, "rows", axis=0, tiled=True)
        right_keys = lax.dynamic_slice_in_dim(all_right, key_start, key_count)
        key_pairs = lax.dynamic_slice_in_dim(all_pairs, key_start, key_count)
        key_geometry = lax.dynamic_slice_in_dim(all_geometry, key_start, key_count)
        key_geometry = key_geometry.reshape(key_count, 3, head_count, point_count - NQP)
        key_heads = key_pairs.reshape(key_count, 2, head_count, head_dim)

        def row_step(inputs):
            return update_row(
                inputs[0],
                inputs[1],
                inputs[2],
                inputs[3],
                inputs[4],
                right_keys,
                dist_embed,
                chain_embed,
                pair_gain,
                mlp_in,
                mlp_bias,
                mlp_out,
            )

        pair_tile = lax.map(
            row_step, (pair_tile, dist_bins[cycle_index], left_proj, pair_mask, same_chain)
        )
        logits = attention_logits(
            triple[:, 0],
            own_points[:, :, :, :NQP],
            key_heads[:, 0],
            key_geometry[:, :, :, :NQP],
            pair_tile,
            key_live,
            bias_weight,
            point_scale,
        )
        row_top = lax.pmax(jnp.max(logits, axis=2), "cols")
        weights = jnp.where(
            key_live[None, None, :], jnp.exp(logits - row_top[:, :, None]), 0.0
        ).astype(jnp.bfloat16)
        row_total = jnp.sum(weights.astype(jnp.float32), axis=2)
        attended = jnp.einsum(
            "ihj,jhd->ihd", weights, key_heads[:, 1], preferred_element_type=jnp.float32
        )
        point_sum = jnp.einsum(
            "ihj,jahp->iahp",
            weights.astype(jnp.float32),
            key_geometry[:, :, :, NQP:],
            precision=HIGHEST,
        )
        pair_sum = jnp.einsum(
            "ihj,ijc->ihc", weights, pair_tile, preferred_element_type=jnp.float32
        )
        row_total, attended, point_sum, pair_sum = (
            lax.psum(row_total.astype(jnp.bfloat16), "cols").astype(jnp.float32),
            lax.psum(attended.reshape(row_count, -1).astype(jnp.bfloat16), "cols").astype(
                jnp.float32
            ),
            lax.psum(point_sum.reshape(row_count, -1).astype(jnp.bfloat16), "cols").astype(
                jnp.float32
            ),
            lax.psum(pair_sum.reshape(row_count, -1).astype(jnp.bfloat16), "cols").astype(
                jnp.float32
            ),
        )
        single, frames = finish_rows(
            single,
            frames,
            row_total,
            attended,
            point_sum,
            pair_sum,
            head_count,
            head_dim,
            value_count,
            channels,
            w_out,
            single_gain,
            w_frame,
        )
    return (pair_tile, single, frames.T)


def solution(mesh):
    in_specs = (
        P(("groups", "rows"), "cols", None),
        P(("groups", "rows"), None),
        P(None, ("groups", "rows")),
        P(None, ("groups", "rows"), "cols"),
        P("groups"),
        P("groups"),
        P(),
        P(),
        P(),
        P(),
        P(),
        P(),
        P(),
        P(),
        P(),
        P(),
        P(),
        P(),
        P(),
        P(),
        P(),
    )
    out_specs = (
        P(("groups", "rows"), "cols", None),
        P(("groups", "rows"), None),
        P(None, ("groups", "rows")),
    )
    return jax.shard_map(shards, mesh=mesh, in_specs=in_specs, out_specs=out_specs, check_vma=False)
```

profile of v0, /device:TPU:0, one launch (start us, length us, event | category | flops | bytes accessed | tf_op | source)
XLA Modules:
  0.0 194.5 jit_solution(276466925991388244)
XLA Ops:
  0.6 0.8 convert_element_type.191
  1.4 0.7 dynamic-slice_convert_fusion
  2.2 0.7 convert_element_type.192
  2.9 1.0 fusion.123
  4.0 1.0 convolution_convert_fusion.9
  5.0 23.2 %all_gather.18 = bf16[128,128]{1,0:T(8,128)(2,1)S(1)} all-gather(bf16[8,128]{1,0:T(8,128)(2,1)S(1)} %convolution_convert_fusion.9), channel_id=1, replica_groups=mesh['groups'=2,'rows'=16,'cols'=1] {'rows'}, dimensions={0}, use_global_device_ids=true | all-gather | bytes 34816 | tf_op jit(solution)/shard_map/all_gather | solution.py:222
  28.3 1.3 slice_bitcast_fusion.8
  29.6 0.7 dynamic_slice.49
  30.3 0.7 broadcast_compare_fusion
  31.1 33.2 %while.20 = (s32[]{:T(128)}, bf16[8,128,128]{1,2,0:T(8,128)(2,1)S(1)}, bf16[8,128,128]{2,1,0:T(8,128)(2,1)}, f32[8,128]{1,0:T(8,128)S(1)}, f32[8,128]{1,0:T(8,12...) while((s32[]{:T(128)}, ...), condition=%wide.region_3.4_spmd, body=%wide.region_0.3_spmd.sunk | while | flops 34556160 | bytes 772905 | solution.py:248
  31.1 0.7 bitcast_convert_fusion.6
  31.9 0.8 constant_dynamic-slice_fusion.8
  32.8 1.0 fusion.202
  33.8 1.5 fusion.203
  35.3 0.7 bitcast_convert_fusion.6
  36.0 0.8 constant_dynamic-slice_fusion.8
  36.9 1.0 fusion.202
  37.9 1.5 fusion.203
  39.4 0.7 bitcast_convert_fusion.6
  40.2 0.8 constant_dynamic-slice_fusion.8
  41.1 1.0 fusion.202
  42.1 1.5 fusion.203
  43.6 0.7 bitcast_convert_fusion.6
  44.4 0.8 constant_dynamic-slice_fusion.8
  45.2 1.0 fusion.202
  46.2 1.5 fusion.203
  47.7 0.7 bitcast_convert_fusion.6
  48.5 0.8 constant_dynamic-slice_fusion.8
  49.4 1.0 fusion.202
  50.4 1.5 fusion.203
  51.9 0.7 bitcast_convert_fusion.6
  52.7 0.8 constant_dynamic-slice_fusion.8
  53.5 1.0 fusion.202
  54.6 1.5 fusion.203
  56.0 0.7 bitcast_convert_fusion.6
  56.8 0.8 constant_dynamic-slice_fusion.8
  57.7 1.0 fusion.202
  58.7 1.5 fusion.203
  60.2 0.7 bitcast_convert_fusion.6
  61.0 0.8 constant_dynamic-slice_fusion.8
  61.9 1.0 fusion.202
  62.9 1.5 fusion.203
  65.9 18.1 %all_gather.20 = f32[128,432]{1,0:T(8,128)S(1)} all-gather(f32[8,432]{1,0:T(8,128)S(1)} %reshape.270), channel_id=1, replica_groups=mesh['groups'=2,'rows'=16,'cols'=1] {'rows'}, dimensions={0}, use_global_device_ids=true | all-gather | bytes 235008 | tf_op jit(solution)/shard_map/all_gather | solution.py:225
  85.2 19.0 %all_gather.19 = bf16[128,384]{1,0:T(8,128)(2,1)S(1)} all-gather(bf16[8,384]{1,0:T(8,128)(2,1)S(1)} %reshape.265), channel_id=1, replica_groups=mesh['groups'=2,'rows'=16,'cols'=1] {'rows'}, dimensions={0}, use_global_device_ids=true | all-gather | bytes 104448 | tf_op jit(solution)/shard_map/all_gather | solution.py:223
  105.8 0.7 copy.80
  107.1 0.7 broadcast_subtract_fusion.1
  107.9 0.9 multiply_reduce_fusion.7
  108.9 0.8 copy.83
  109.6 1.0 fusion.92
  110.6 0.8 concatenate.11
  111.4 1.1 fusion.118
  113.1 17.6 %all_gather.21 = bf16[128,128]{1,0:T(8,128)(2,1)S(1)} all-gather(bf16[8,128]{1,0:T(8,128)(2,1)S(1)} %convolution_convert_fusion.8), channel_id=1, replica_groups=mesh['groups'=2,'rows'=16,'cols'=1] {'rows'}, dimensions={0}, use_global_device_ids=true | all-gather | bytes 34816 | tf_op jit(solution)/shard_map/all_gather | solution.py:222
  130.9 17.7 %while.21 = (s32[]{:T(128)}, bf16[8,128,128]{1,2,0:T(8,128)(2,1)S(1)}, bf16[8,128,128]{1,2,0:T(8,128)(2,1)S(1)}, f32[8,128]{1,0:T(8,128)}, f32[8,128]{1,0:T(8,12...) while((s32[]{:T(128)}, ...), condition=%wide.region_14.15_spmd, body=%wide.region_11.14_spmd.sunk | while | flops 34556160 | bytes 641833 | solution.py:248
  131.0 0.7 fusion.207
  133.2 0.7 fusion.207
  135.4 0.7 fusion.207
  137.6 0.7 fusion.207
  139.8 0.7 fusion.207
  142.1 0.7 fusion.207
  144.3 0.7 fusion.207
  146.5 0.7 fusion.207
  148.7 0.9 copy.108
  151.5 19.4 %all_gather.23 = f32[128,432]{1,0:T(8,128)S(1)} all-gather(f32[8,432]{1,0:T(8,128)S(1)} %reshape.281), channel_id=1, replica_groups=mesh['groups'=2,'rows'=16,'cols'=1] {'rows'}, dimensions={0}, use_global_device_ids=true | all-gather | bytes 235008 | tf_op jit(solution)/shard_map/all_gather | solution.py:225
  172.0 17.8 %all_gather.22 = bf16[128,384]{1,0:T(8,128)(2,1)S(1)} all-gather(bf16[8,384]{1,0:T(8,128)(2,1)S(1)} %reshape.276), channel_id=1, replica_groups=mesh['groups'=2,'rows'=16,'cols'=1] {'rows'}, dimensions={0}, use_global_device_ids=true | all-gather | bytes 104448 | tf_op jit(solution)/shard_map/all_gather | solution.py:223
  (299 shorter events, 26.5 us)
Async XLA Ops:
  0.6 110.8 %copy-start = (bf16[2112,384]{1,0:T(8,128)(2,1)S(1)}, bf16[2112,384]{1,0:T(8,128)(2,1)}, u32[]{:S(2)}) copy-start(bf16[2112,384]{1,0:T(8,128)(2,1)} %param.43) | copy-start | bytes 4866052
  31.1 33.3 %copy-start.25 = (s32[128]{0:T(128)S(1)}, s32[128]{0:T(128)}, u32[]{:S(2)}) copy-start(s32[128]{0:T(128)} %param.29) | copy-start | bytes 1540
  31.1 33.3 %copy-start.3 = (bf16[384,576]{0,1:T(8,128)(2,1)S(1)}, bf16[384,576]{0,1:T(8,128)(2,1)}, u32[]{:S(2)}) copy-start(bf16[384,576]{0,1:T(8,128)(2,1)} %param.40) | copy-start | bytes 1327108
  31.1 33.6 %copy-start.19 = (f32[12,8]{0,1:T(8,128)S(1)}, f32[12,8]{0,1:T(8,128)}, u32[]{:S(2)}) copy-start(f32[12,8]{0,1:T(8,128)} %param.27) | copy-start | bytes 1156
  64.3 0.9 copy-start.12
  64.4 0.9 copy-start.22
  64.4 40.2 %copy-start.27 = (pred[128]{0:T(512)(128)(4,1)}, pred[128]{0:T(512)(128)(4,1)S(1)}, u32[]{:S(2)}) copy-start(pred[128]{0:T(512)(128)(4,1)S(1)} %broadcast_compare_fusion.1) | copy-start | bytes 388
  64.6 19.7 %copy-start.26 = (f32[12]{0:T(128)S(1)}, f32[12]{0:T(128)}, u32[]{:S(2)}) copy-start(f32[12]{0:T(128)} %param.42) | copy-start | bytes 148
  64.9 42.0 %copy-start.15 = (f32[8,3]{0,1:T(4,128)}, f32[8,3]{0,1:T(4,128)S(1)}, u32[]{:S(2)}) copy-start(f32[8,3]{0,1:T(4,128)S(1)} %slice.143) | copy-start | bytes 292
  65.3 19.5 %copy-start.4 = (bf16[384,576]{0,1:T(8,128)(2,1)S(1)}, bf16[384,576]{0,1:T(8,128)(2,1)}, u32[]{:S(2)}) copy-start(bf16[384,576]{0,1:T(8,128)(2,1)} %param.39) | copy-start | bytes 1327108
  65.8 38.6 %copy-start.17 = (bf16[128,12]{0,1:T(8,128)(2,1)S(1)}, bf16[128,12]{0,1:T(8,128)(2,1)}, u32[]{:S(2)}) copy-start(bf16[128,12]{0,1:T(8,128)(2,1)} %param.41) | copy-start | bytes 9220
  84.4 0.9 copy-start.20
  104.9 1.8 copy-start.29
  104.9 2.0 %copy-start.16 = (bf16[8,12]{0,1:T(8,128)(2,1)}, bf16[8,12]{0,1:T(8,128)(2,1)S(1)}, u32[]{:S(2)}) copy-start(bf16[8,12]{0,1:T(8,128)(2,1)S(1)} %get-tuple-element.307) | copy-start | bytes 580
  106.7 6.1 %copy-start.13 = (f32[384]{0:T(512)S(1)}, f32[384]{0:T(512)}, u32[]{:S(2)}) copy-start(f32[384]{0:T(512)} %param.44) | copy-start | bytes 4612
  106.7 6.1 %copy-start.5 = (bf16[384,128]{1,0:T(8,128)(2,1)S(1)}, bf16[384,128]{1,0:T(8,128)(2,1)}, u32[]{:S(2)}) copy-start(bf16[384,128]{1,0:T(8,128)(2,1)} %param.31) | copy-start | bytes 294916
  106.7 6.3 %copy-start.6 = (bf16[384,128]{1,0:T(8,128)(2,1)S(1)}, bf16[384,128]{1,0:T(8,128)(2,1)}, u32[]{:S(2)}) copy-start(bf16[384,128]{1,0:T(8,128)(2,1)} %param.32) | copy-start | bytes 294916
  106.9 23.9 %copy-start.1 = (bf16[128,512]{1,0:T(8,128)(2,1)S(1)}, bf16[128,512]{1,0:T(8,128)(2,1)}, u32[]{:S(2)}) copy-start(bf16[128,512]{1,0:T(8,128)(2,1)} %get-tuple-element.600) | copy-start | bytes 393220
  106.9 23.9 %copy-start.2 = (bf16[512,128]{1,0:T(8,128)(2,1)S(1)}, bf16[512,128]{1,0:T(8,128)(2,1)}, u32[]{:S(2)}) copy-start(bf16[512,128]{1,0:T(8,128)(2,1)} %get-tuple-element.601) | copy-start | bytes 393220
  106.9 23.9 %copy-start.7 = (f32[512]{0:T(512)S(1)}, f32[512]{0:T(512)}, u32[]{:S(2)}) copy-start(f32[512]{0:T(512)} %get-tuple-element.602) | copy-start | bytes 6148
  107.0 23.9 %copy-start.8 = (bf16[2,128]{1,0:T(2,128)(2,1)S(1)}, bf16[2,128]{1,0:T(2,128)(2,1)}, u32[]{:S(2)}) copy-start(bf16[2,128]{1,0:T(2,128)(2,1)} %get-tuple-element.603) | copy-start | bytes 1540
  107.0 23.9 %copy-start.9 = (f32[128]{0:T(128)S(1)}, f32[128]{0:T(128)}, u32[]{:S(2)}) copy-start(f32[128]{0:T(128)} %get-tuple-element.604) | copy-start | bytes 1540
  107.1 23.8 %copy-start.23 = (pred[8,128]{1,0:T(8,128)(4,1)S(1)}, pred[8,128]{1,0:T(8,128)(4,1)}, u32[]{:S(2)}) copy-start(pred[8,128]{1,0:T(8,128)(4,1)} %copy-done.22) | copy-start | bytes 3076
  107.1 23.8 %copy-start.24 = (bf16[15,128]{1,0:T(8,128)(2,1)S(1)}, bf16[15,128]{1,0:T(8,128)(2,1)}, u32[]{:S(2)}) copy-start(bf16[15,128]{1,0:T(8,128)(2,1)} %get-tuple-element.607) | copy-start | bytes 11524
  130.9 18.6 %copy-start.11 = (bf16[384,6]{0,1:T(8,128)(2,1)S(1)}, bf16[384,6]{0,1:T(8,128)(2,1)}, u32[]{:S(2)}) copy-start(bf16[384,6]{0,1:T(8,128)(2,1)} %param.45) | copy-start | bytes 13828
  150.3 20.9 %copy-start.21 = (f32[12]{0:T(128)S(1)}, f32[12]{0:T(128)}, u32[]{:S(2)}) copy-start(f32[12]{0:T(128)} %copy-done.20) | copy-start | bytes 148
  151.3 38.7 %copy-start.18 = (bf16[128,12]{0,1:T(8,128)(2,1)S(1)}, bf16[128,12]{0,1:T(8,128)(2,1)}, u32[]{:S(2)}) copy-start(bf16[128,12]{0,1:T(8,128)(2,1)} %param.41) | copy-start | bytes 9220
  151.4 38.7 %copy-start.28 = (pred[128]{0:T(512)(128)(4,1)S(1)}, pred[128]{0:T(512)(128)(4,1)}, u32[]{:S(2)}) copy-start(pred[128]{0:T(512)(128)(4,1)} %copy-done.27) | copy-start | bytes 388
  172.0 20.1 %copy-start.14 = (f32[384]{0:T(512)S(1)}, f32[384]{0:T(512)}, u32[]{:S(2)}) copy-start(f32[384]{0:T(512)} %param.44) | copy-start | bytes 4612
  192.8 1.7 copy-start.10
where the time goes:
time: 197 us; the launch traced here: 195 us
  blocking collectives  115 us (58%)
  matrix products  35.8 us (18%)
  local copies, waits for them, and re-layouts  30 us (15%)
  other arithmetic  11.5 us (6%)
    all_gather x2, blocking collectives, shards(): lax.all_gather(own_right, 'rows', axis=0, tiled=True)  40.7 us
    all_gather x2, blocking collectives, shards(): all_geometry = lax.all_gather(own_geometry, 'rows', axis=0, tiled=True)  37.6 us
    all_gather x2, blocking collectives, shards(): lax.all_gather(own_pairs, 'rows', axis=0, tiled=True)  36.8 us
    dot_general x16, matrix products, update_row(): mixed_out = jnp.dot(hidden, mlp_out, preferred_element_type=jnp.float32)  15.4 us
    dot_general x16, matrix products, update_row(): looked = jnp.dot(onehot, dist_embed, preferred_element_type=jnp.float32)  9.72 us
    dynamic_slice x16, local copies, waits for them, and re-layouts, shards(): lax.map(row_step, (pair_tile, dist_bins[cycle_index], left_proj, pair_mas...  7.02 us
    convert_element_type x16, other arithmetic, update_row(): chain_embed[1].astype(jnp.float32)  5.94 us
    eq x16, local copies, waits for them, and re-layouts, update_row(): bins_row[:, None]  5.66 us

commit v1 on v0

--- a/solution.py
+++ b/solution.py
@@ -222,7 +222,18 @@
             lax.all_gather(own_right, "rows", axis=0, tiled=True),
             lax.all_gather(own_pairs, "rows", axis=0, tiled=True),
         )
-        all_geometry = lax.all_gather(own_geometry, "rows", axis=0, tiled=True)
+        ways = lax.axis_size("rows")
+        up = [(d, (d + 1) % ways) for d in range(ways)]
+        down = [(d, (d - 1) % ways) for d in range(ways)]
+        earlier, later = ([own_geometry], [own_geometry])
+        for _ in range(ways // 2):
+            earlier.append(lax.ppermute(earlier[-1], "rows", up))
+        for _ in range((ways - 1) // 2):
+            later.append(lax.ppermute(later[-1], "rows", down))
+        line = jnp.concatenate([*earlier[::-1], *later[1:]], axis=0)
+        all_geometry = jnp.roll(
+            line, (lax.axis_index("rows") - ways // 2) * own_geometry.shape[0], axis=0
+        )
         right_keys = lax.dynamic_slice_in_dim(all_right, key_start, key_count)
         key_pairs = lax.dynamic_slice_in_dim(all_pairs, key_start, key_count)
         key_geometry = lax.dynamic_slice_in_dim(all_geometry, key_start, key_count)

time: 197 us -> 218 us (1.11)
  starting transfers between devices: 0 us -> 54.2 us
  blocking collectives: 115 us -> 73.9 us
  waiting for transfers between devices: 0 us -> 17.3 us
  matrix products: 35.8 us -> 27.6 us
  other arithmetic: 11.5 us -> 5.43 us
  local copies, waits for them, and re-layouts: 30 us -> 34.8 us
    ppermute x0 -> x30, starting transfers between devices: none -> 54.2 us  [the longest x14 52.4 us: shards(): later.append(lax.ppermute(later[-1], 'rows', down))]
    all_gather x2 -> x0, blocking collectives: 37.6 us -> none  [shards(): all_geometry = lax.all_gather(own_geometry, 'rows', axis=0, tiled=True)]
    ppermute x0 -> x30, waiting for transfers between devices: none -> 17.3 us  [the longest x16 10.5 us: shards(): earlier.append(lax.ppermute(earlier[-1], 'rows', up))]
    dot_general x16, matrix products: 15.4 us -> 7.39 us  [update_row(): mixed_out = jnp.dot(hidden, mlp_out, preferred_element_type=jnp.float32)]
    convert_element_type x16, other arithmetic: 5.94 us -> 0.08 us  [update_row(): chain_embed[1].astype(jnp.float32)]
    broadcast_in_dim x16, local copies, waits for them, and re-layouts: 0.16 us -> 5.44 us  [update_row(): jnp.where(same_row[:, None], chain_embed[1].astype(jnp.float32), chain_em...]
    all_gather x2, blocking collectives: 40.7 us -> 37.4 us  [shards(): lax.all_gather(own_right, 'rows', axis=0, tiled=True)]
  transfers between devices with their start and end apart: 0 -> 30, of which waited for: 0 -> 14; matrix products, arithmetic and copies ran while one was open for 0% -> 23% of each run, Pallas kernels for 0% -> 0%
where the time goes in v1:
time: 218 us; the launch traced here: 216 us
  blocking collectives  73.9 us (34%)
  starting transfers between devices  54.2 us (25%)
  local copies, waits for them, and re-layouts  34.8 us (16%)
  matrix products  27.6 us (13%)
  waiting for transfers between devices  17.3 us (8%)
  other arithmetic  5.43 us (2%)
    ppermute x14, starting transfers between devices, shards(): later.append(lax.ppermute(later[-1], 'rows', down))  52.4 us
    all_gather x2, blocking collectives, shards(): lax.all_gather(own_right, 'rows', axis=0, tiled=True)  37.4 us
    all_gather x2, blocking collectives, shards(): lax.all_gather(own_pairs, 'rows', axis=0, tiled=True)  36.5 us
    ppermute x16, waiting for transfers between devices, shards(): earlier.append(lax.ppermute(earlier[-1], 'rows', up))  10.5 us
    dot_general x16, matrix products, update_row(): looked = jnp.dot(onehot, dist_embed, preferred_element_type=jnp.float32)  9.63 us
    dot_general x16, matrix products, update_row(): mixed_out = jnp.dot(hidden, mlp_out, preferred_element_type=jnp.float32)  7.39 us
    dynamic_slice x16, local copies, waits for them, and re-layouts, shards(): lax.map(row_step, (pair_tile, dist_bins[cycle_index], left_proj, pair_mas...  7.06 us
    ppermute x14, waiting for transfers between devices, shards(): later.append(lax.ppermute(later[-1], 'rows', down))  6.78 us
  transfers between devices with their start and end apart: 30, of which 14 were waited for; matrix products, arithmetic and copies ran while one was open for 23% of the time, Pallas kernels for 0%

profile of v1, /device:TPU:0, one launch (start us, length us, event | category | flops | bytes accessed | tf_op | source)
XLA Modules:
  0.0 215.7 jit_solution(17448987245354460827)
XLA Ops:
  0.8 0.9 copy.68
  1.8 0.7 convert_element_type.192
  2.5 1.2 fusion.126
  5.1 5.0 %collective-permute-start.8 = (f32[8,432]{1,0:T(8,128)S(1)}, f32[8,432]{1,0:T(8,128)S(1)}, u32[]{:S(2)}, u32[]{:S(2)}) collective-permute-start(f32[8,432]{1,0:T(8,128)S(1)} %reshape.270), channel_id=1, source_target_pairs={{0,15},{1,0},{2,1},{3,2},{4,3},{5,4},{6,5},{7,6},{8,7},{9,8},{10,9... | collective-permute-start | bytes 41480 | tf_op jit(solution)/shard_map/ppermute | solution.py:232
  11.3 19.4 %all_gather.12 = bf16[128,128]{1,0:T(8,128)(2,1)S(1)} all-gather(bf16[8,128]{1,0:T(8,128)(2,1)S(1)} %convolution_convert_fusion.9), channel_id=1, replica_groups=mesh['groups'=2,'rows'=16,'cols'=1] {'rows'}, dimensions={0}, use_global_device_ids=true | all-gather | bytes 34816 | tf_op jit(solution)/shard_map/all_gather | solution.py:222
  31.3 14.0 %while.20 = (s32[]{:T(128)}, bf16[8,128,128]{1,2,0:T(8,128)(2,1)S(1)}, bf16[8,128,128]{2,1,0:T(8,128)(2,1)}, f32[8,128]{1,0:T(8,128)S(1)}, f32[8,128]{1,0:T(8,12...) while((s32[]{:T(128)}, ...), condition=%wide.region_3.4_spmd, body=%wide.region_0.3_spmd.sunk | while | flops 34556160 | bytes 772897 | solution.py:259
  31.3 0.8 constant_dynamic-slice_fusion.8
  33.1 0.8 constant_dynamic-slice_fusion.8
  34.9 0.8 constant_dynamic-slice_fusion.8
  36.6 0.8 constant_dynamic-slice_fusion.8
  38.4 0.8 constant_dynamic-slice_fusion.8
  40.1 0.8 constant_dynamic-slice_fusion.8
  41.8 0.8 constant_dynamic-slice_fusion.8
  43.6 0.8 constant_dynamic-slice_fusion.8
  45.6 4.5 %collective-permute-start.9 = (f32[8,432]{1,0:T(8,128)S(1)}, f32[8,432]{1,0:T(8,128)S(1)}, u32[]{:S(2)}, u32[]{:S(2)}) collective-permute-start(f32[8,432]{1,0:T(8,128)S(1)} %collective-permute-done.8), channel_id=1, source_target_pairs={{0,15},{1,0},{2,1},{3,2},{4,3},{5,4},{6,5},{7,6},{8,7},{9,8},{10,9... | collective-permute-start | bytes 41480 | tf_op jit(solution)/shard_map/ppermute | solution.py:232
  50.1 1.2 collective-permute-done.2
  51.3 0.8 fusion.114
  52.0 4.4 %collective-permute-start.10 = (f32[8,432]{1,0:T(8,128)S(1)}, f32[8,432]{1,0:T(8,128)S(1)}, u32[]{:S(2)}, u32[]{:S(2)}) collective-permute-start(f32[8,432]{1,0:T(8,128)S(1)} %collective-permute-done.9), channel_id=1, source_target_pairs={{0,15},{1,0},{2,1},{3,2},{4,3},{5,4},{6,5},{7,6},{8,7},{9,8},{10,9... | collective-permute-start | bytes 41480 | tf_op jit(solution)/shard_map/ppermute | solution.py:232
  57.9 4.4 %collective-permute-start.11 = (f32[8,432]{1,0:T(8,128)S(1)}, f32[8,432]{1,0:T(8,128)S(1)}, u32[]{:S(2)}, u32[]{:S(2)}) collective-permute-start(f32[8,432]{1,0:T(8,128)S(1)} %collective-permute-done.10), channel_id=1, source_target_pairs={{0,15},{1,0},{2,1},{3,2},{4,3},{5,4},{6,5},{7,6},{8,7},{9,8},{10,9... | collective-permute-start | bytes 41480 | tf_op jit(solution)/shard_map/ppermute | solution.py:232
  63.8 4.5 %collective-permute-start.12 = (f32[8,432]{1,0:T(8,128)S(1)}, f32[8,432]{1,0:T(8,128)S(1)}, u32[]{:S(2)}, u32[]{:S(2)}) collective-permute-start(f32[8,432]{1,0:T(8,128)S(1)} %collective-permute-done.11), channel_id=1, source_target_pairs={{0,15},{1,0},{2,1},{3,2},{4,3},{5,4},{6,5},{7,6},{8,7},{9,8},{10,9... | collective-permute-start | bytes 41480 | tf_op jit(solution)/shard_map/ppermute | solution.py:232
  69.7 4.4 %collective-permute-start.13 = (f32[8,432]{1,0:T(8,128)S(1)}, f32[8,432]{1,0:T(8,128)S(1)}, u32[]{:S(2)}, u32[]{:S(2)}) collective-permute-start(f32[8,432]{1,0:T(8,128)S(1)} %collective-permute-done.12), channel_id=1, source_target_pairs={{0,15},{1,0},{2,1},{3,2},{4,3},{5,4},{6,5},{7,6},{8,7},{9,8},{10,9... | collective-permute-start | bytes 41480 | tf_op jit(solution)/shard_map/ppermute | solution.py:232
  74.7 18.2 %all_gather.13 = bf16[128,384]{1,0:T(8,128)(2,1)S(1)} all-gather(bf16[8,384]{1,0:T(8,128)(2,1)S(1)} %reshape.265), channel_id=1, replica_groups=mesh['groups'=2,'rows'=16,'cols'=1] {'rows'}, dimensions={0}, use_global_device_ids=true | all-gather | bytes 104448 | tf_op jit(solution)/shard_map/all_gather | solution.py:223
  93.6 0.7 copy.80
  94.4 1.2 collective-permute-start.14
  95.8 1.3 collective-permute-done.14
  97.8 1.1 fusion.119
  99.0 0.9 fusion.51
  100.4 1.1 copy.78
  103.2 0.8 fusion.109
  104.0 0.8 fusion.128
  107.0 0.8 collective-permute-start.15
  107.7 3.8 %collective-permute-start.23 = (f32[8,432]{1,0:T(8,128)S(1)}, f32[8,432]{1,0:T(8,128)S(1)}, u32[]{:S(2)}, u32[]{:S(2)}) collective-permute-start(f32[8,432]{1,0:T(8,128)S(1)} %reshape.281), channel_id=1, source_target_pairs={{0,15},{1,0},{2,1},{3,2},{4,3},{5,4},{6,5},{7,6},{8,7},{9,8},{10,9... | collective-permute-start | bytes 41480 | tf_op jit(solution)/shard_map/ppermute | solution.py:232
  111.6 1.2 collective-permute-done.15
  113.0 5.7 %collective-permute-done.16 = f32[8,432]{1,0:T(8,128)S(1)} collective-permute-done((f32[8,432]{1,0:T(8,128)S(1)}, f32[8,432]{1,0:T(8,128)S(1)}, u32[]{:S(2)}, u32[]{:S(2)}) %collective-permute-start.16) | collective-permute-done | bytes 13856 | tf_op jit(solution)/shard_map/ppermute | solution.py:230
  118.7 18.1 %all_gather.14 = bf16[128,128]{1,0:T(8,128)(2,1)S(1)} all-gather(bf16[8,128]{1,0:T(8,128)(2,1)S(1)} %convolution_convert_fusion.8), channel_id=1, replica_groups=mesh['groups'=2,'rows'=16,'cols'=1] {'rows'}, dimensions={0}, use_global_device_ids=true | all-gather | bytes 34816 | tf_op jit(solution)/shard_map/all_gather | solution.py:222
  136.9 1.2 collective-permute-start.24
  138.2 28.3 %while.21 = (s32[]{:T(128)}, bf16[8,128,128]{1,2,0:T(8,128)(2,1)S(1)}, bf16[8,128,128]{1,2,0:T(8,128)(2,1)S(1)}, f32[8,128]{1,0:T(8,128)}, f32[8,128]{1,0:T(8,12...) while((s32[]{:T(128)}, ...), condition=%wide.region_14.16_spmd, body=%wide.region_11.15_spmd.sunk | while | flops 34556160 | bytes 641825 | solution.py:259
  138.3 0.7 fusion.210
  140.3 0.9 fusion.211
  141.8 0.7 fusion.210
  143.9 0.9 fusion.211
  145.3 0.7 fusion.210
  147.4 0.9 fusion.211
  148.9 0.7 fusion.210
  150.9 0.9 fusion.211
  152.4 0.7 fusion.210
  154.5 0.9 fusion.211
  155.9 0.7 fusion.210
  158.0 0.9 fusion.211
  159.5 0.7 fusion.210
  161.5 0.9 fusion.211
  163.0 0.7 fusion.210
  165.1 0.9 fusion.211
  166.6 4.5 %collective-permute-start.25 = (f32[8,432]{1,0:T(8,128)S(1)}, f32[8,432]{1,0:T(8,128)S(1)}, u32[]{:S(2)}, u32[]{:S(2)}) collective-permute-start(f32[8,432]{1,0:T(8,128)S(1)} %collective-permute-done.24), channel_id=1, source_target_pairs={{0,15},{1,0},{2,1},{3,2},{4,3},{5,4},{6,5},{7,6},{8,7},{9,8},{10,9... | collective-permute-start | bytes 41480 | tf_op jit(solution)/shard_map/ppermute | solution.py:232
  171.3 1.2 collective-permute-done.25
  172.5 4.4 %collective-permute-start.26 = (f32[8,432]{1,0:T(8,128)S(1)}, f32[8,432]{1,0:T(8,128)S(1)}, u32[]{:S(2)}, u32[]{:S(2)}) collective-permute-start(f32[8,432]{1,0:T(8,128)S(1)} %collective-permute-done.25), channel_id=1, source_target_pairs={{0,15},{1,0},{2,1},{3,2},{4,3},{5,4},{6,5},{7,6},{8,7},{9,8},{10,9... | collective-permute-start | bytes 41480 | tf_op jit(solution)/shard_map/ppermute | solution.py:232
  177.4 1.0 collective-permute-done.26
  178.4 4.4 %collective-permute-start.27 = (f32[8,432]{1,0:T(8,128)S(1)}, f32[8,432]{1,0:T(8,128)S(1)}, u32[]{:S(2)}, u32[]{:S(2)}) collective-permute-start(f32[8,432]{1,0:T(8,128)S(1)} %collective-permute-done.26), channel_id=1, source_target_pairs={{0,15},{1,0},{2,1},{3,2},{4,3},{5,4},{6,5},{7,6},{8,7},{9,8},{10,9... | collective-permute-start | bytes 41480 | tf_op jit(solution)/shard_map/ppermute | solution.py:232
  183.1 1.1 collective-permute-done.27
  184.2 4.4 %collective-permute-start.28 = (f32[8,432]{1,0:T(8,128)S(1)}, f32[8,432]{1,0:T(8,128)S(1)}, u32[]{:S(2)}, u32[]{:S(2)}) collective-permute-start(f32[8,432]{1,0:T(8,128)S(1)} %collective-permute-done.27), channel_id=1, source_target_pairs={{0,15},{1,0},{2,1},{3,2},{4,3},{5,4},{6,5},{7,6},{8,7},{9,8},{10,9... | collective-permute-start | bytes 41480 | tf_op jit(solution)/shard_map/ppermute | solution.py:232
  188.7 18.2 %all_gather.15 = bf16[128,384]{1,0:T(8,128)(2,1)S(1)} all-gather(bf16[8,384]{1,0:T(8,128)(2,1)S(1)} %reshape.276), channel_id=1, replica_groups=mesh['groups'=2,'rows'=16,'cols'=1] {'rows'}, dimensions={0}, use_global_device_ids=true | all-gather | bytes 104448 | tf_op jit(solution)/shard_map/all_gather | solution.py:223
  206.9 0.8 copy.108
  207.9 1.2 collective-permute-start.29
  209.3 1.3 collective-permute-done.29
  (421 shorter events, 43.0 us)
Async XLA Ops:
  0.6 101.5 %copy-start = (bf16[2112,384]{1,0:T(8,128)(2,1)S(1)}, bf16[2112,384]{1,0:T(8,128)(2,1)}, u32[]{:S(2)}) copy-start(bf16[2112,384]{1,0:T(8,128)(2,1)} %param.45) | copy-start | bytes 4866052
  0.6 9.4 %copy-start.42 = (s32[128]{0:T(128)S(1)}, s32[128]{0:T(128)}, u32[]{:S(2)}) copy-start(s32[128]{0:T(128)} %param.31) | copy-start | bytes 1540
  0.7 9.5 %copy-start.40 = (s32[128]{0:T(128)S(1)}, s32[128]{0:T(128)}, u32[]{:S(2)}) copy-start(s32[128]{0:T(128)} %param.32) | copy-start | bytes 1540
  0.7 9.6 %copy-start.6 = (bf16[384,128]{1,0:T(8,128)(2,1)S(1)}, bf16[384,128]{1,0:T(8,128)(2,1)}, u32[]{:S(2)}) copy-start(bf16[384,128]{1,0:T(8,128)(2,1)} %param.34) | copy-start | bytes 294916
  0.7 9.8 %copy-start.5 = (bf16[384,128]{1,0:T(8,128)(2,1)S(1)}, bf16[384,128]{1,0:T(8,128)(2,1)}, u32[]{:S(2)}) copy-start(bf16[384,128]{1,0:T(8,128)(2,1)} %param.33) | copy-start | bytes 294916
  0.7 9.9 %copy-start.32 = (s32[2,8,128]{2,1,0:T(8,128)S(1)}, s32[2,8,128]{2,1,0:T(8,128)}, u32[]{:S(2)}) copy-start(s32[2,8,128]{2,1,0:T(8,128)} %param.30) | copy-start | bytes 24580
  0.7 30.5 %copy-start.41 = (bf16[15,128]{1,0:T(8,128)(2,1)S(1)}, bf16[15,128]{1,0:T(8,128)(2,1)}, u32[]{:S(2)}) copy-start(bf16[15,128]{1,0:T(8,128)(2,1)} %param.35) | copy-start | bytes 11524
  0.7 30.5 %copy-start.9 = (bf16[2,128]{1,0:T(2,128)(2,1)S(1)}, bf16[2,128]{1,0:T(2,128)(2,1)}, u32[]{:S(2)}) copy-start(bf16[2,128]{1,0:T(2,128)(2,1)} %param.36) | copy-start | bytes 1540
  0.7 30.5 %copy-start.15 = (f32[128]{0:T(128)S(1)}, f32[128]{0:T(128)}, u32[]{:S(2)}) copy-start(f32[128]{0:T(128)} %param.37) | copy-start | bytes 1540
  0.7 30.5 %copy-start.1 = (bf16[128,512]{1,0:T(8,128)(2,1)S(1)}, bf16[128,512]{1,0:T(8,128)(2,1)}, u32[]{:S(2)}) copy-start(bf16[128,512]{1,0:T(8,128)(2,1)} %param.38) | copy-start | bytes 393220
  0.7 30.5 %copy-start.8 = (f32[512]{0:T(512)S(1)}, f32[512]{0:T(512)}, u32[]{:S(2)}) copy-start(f32[512]{0:T(512)} %param.39) | copy-start | bytes 6148
  0.8 30.5 %copy-start.2 = (bf16[512,128]{1,0:T(8,128)(2,1)S(1)}, bf16[512,128]{1,0:T(8,128)(2,1)}, u32[]{:S(2)}) copy-start(bf16[512,128]{1,0:T(8,128)(2,1)} %param.40) | copy-start | bytes 393220
  1.7 91.9 %copy-start.12 = (f32[8,3,3]{0,2,1:T(4,128)}, f32[8,3,3]{0,2,1:T(4,128)S(1)}, u32[]{:S(2)}) copy-start(f32[8,3,3]{0,2,1:T(4,128)S(1)} %reshape.268) | copy-start | bytes 868
  1.8 29.4 %copy-start.10 = (f32[8,3,3]{2,1,0:T(4,128)}, f32[8,3,3]{2,1,0:T(4,128)S(1)}, u32[]{:S(2)}) copy-start(f32[8,3,3]{2,1,0:T(4,128)S(1)} %copy.69) | copy-start | bytes 868
  4.5 26.2 %collective-permute-start = (f32[8,432]{1,0:T(8,128)S(1)}, f32[8,432]{1,0:T(8,128)S(1)}, u32[]{:S(2)}, u32[]{:S(2)}) collective-permute-start(f32[8,432]{1,0:T(8,128)S(1)} %reshape.270), channel_id=1, source_target_pairs={{0,1},{1,2},{2,3},{3,4},{4,5},{5,6},{6,7},{7,8},{8,9},{9,10},{10,1... | collective-permute-start | bytes 41480 | tf_op jit(solution)/shard_map/ppermute | solution.py:230
  5.1 40.6 %collective-permute-start.8 = (f32[8,432]{1,0:T(8,128)S(1)}, f32[8,432]{1,0:T(8,128)S(1)}, u32[]{:S(2)}, u32[]{:S(2)}) collective-permute-start(f32[8,432]{1,0:T(8,128)S(1)} %reshape.270), channel_id=1, source_target_pairs={{0,15},{1,0},{2,1},{3,2},{4,3},{5,4},{6,5},{7,6},{8,7},{9,8},{10,9... | collective-permute-start | bytes 41480 | tf_op jit(solution)/shard_map/ppermute | solution.py:232
  30.8 14.6 %collective-permute-start.1 = (f32[8,432]{1,0:T(8,128)S(1)}, f32[8,432]{1,0:T(8,128)S(1)}, u32[]{:S(2)}, u32[]{:S(2)}) collective-permute-start(f32[8,432]{1,0:T(8,128)S(1)} %collective-permute-done), channel_id=1, source_target_pairs={{0,1},{1,2},{2,3},{3,4},{4,5},{5,6},{6,7},{7,8},{8,9},{9,10},{10,1... | collective-permute-start | bytes 41480 | tf_op jit(solution)/shard_map/ppermute | solution.py:230
  31.3 14.1 %copy-start.4 = (bf16[384,576]{0,1:T(8,128)(2,1)S(1)}, bf16[384,576]{0,1:T(8,128)(2,1)}, u32[]{:S(2)}) copy-start(bf16[384,576]{0,1:T(8,128)(2,1)} %param.41) | copy-start | bytes 1327108
  31.3 20.0 %copy-start.30 = (bf16[128,12]{0,1:T(8,128)(2,1)S(1)}, bf16[128,12]{0,1:T(8,128)(2,1)}, u32[]{:S(2)}) copy-start(bf16[128,12]{0,1:T(8,128)(2,1)} %param.43) | copy-start | bytes 9220
  31.3 31.7 %copy-start.43 = (f32[12]{0:T(128)S(1)}, f32[12]{0:T(128)}, u32[]{:S(2)}) copy-start(f32[12]{0:T(128)} %param.44) | copy-start | bytes 148
  45.3 18.2 %copy-start.22 = (f32[8,128]{1,0:T(8,128)}, f32[8,128]{1,0:T(8,128)S(1)}, u32[]{:S(2)}) copy-start(f32[8,128]{1,0:T(8,128)S(1)} %get-tuple-element.610) | copy-start | bytes 12292
  45.3 18.2 %copy-start.39 = (pred[8,128]{1,0:T(8,128)(4,1)}, pred[8,128]{1,0:T(8,128)(4,1)S(1)}, u32[]{:S(2)}) copy-start(pred[8,128]{1,0:T(8,128)(4,1)S(1)} %get-tuple-element.667) | copy-start | bytes 3076
  45.3 5.9 %collective-permute-start.2 = (f32[8,432]{1,0:T(8,128)S(1)}, f32[8,432]{1,0:T(8,128)S(1)}, u32[]{:S(2)}, u32[]{:S(2)}) collective-permute-start(f32[8,432]{1,0:T(8,128)S(1)} %collective-permute-done.1), channel_id=1, source_target_pairs={{0,1},{1,2},{2,3},{3,4},{4,5},{5,6},{6,7},{7,8},{8,9},{9,10},{10,1... | collective-permute-start | bytes 41480 | tf_op jit(solution)/shard_map/ppermute | solution.py:230
  45.6 6.4 %collective-permute-start.9 = (f32[8,432]{1,0:T(8,128)S(1)}, f32[8,432]{1,0:T(8,128)S(1)}, u32[]{:S(2)}, u32[]{:S(2)}) collective-permute-start(f32[8,432]{1,0:T(8,128)S(1)} %collective-permute-done.8), channel_id=1, source_target_pairs={{0,15},{1,0},{2,1},{3,2},{4,3},{5,4},{6,5},{7,6},{8,7},{9,8},{10,9... | collective-permute-start | bytes 41480 | tf_op jit(solution)/shard_map/ppermute | solution.py:232
  51.3 5.9 %collective-permute-start.3 = (f32[8,432]{1,0:T(8,128)S(1)}, f32[8,432]{1,0:T(8,128)S(1)}, u32[]{:S(2)}, u32[]{:S(2)}) collective-permute-start(f32[8,432]{1,0:T(8,128)S(1)} %collective-permute-done.2), channel_id=1, source_target_pairs={{0,1},{1,2},{2,3},{3,4},{4,5},{5,6},{6,7},{7,8},{8,9},{9,10},{10,1... | collective-permute-start | bytes 41480 | tf_op jit(solution)/shard_map/ppermute | solution.py:230
  52.0 5.9 %collective-permute-start.10 = (f32[8,432]{1,0:T(8,128)S(1)}, f32[8,432]{1,0:T(8,128)S(1)}, u32[]{:S(2)}, u32[]{:S(2)}) collective-permute-start(f32[8,432]{1,0:T(8,128)S(1)} %collective-permute-done.9), channel_id=1, source_target_pairs={{0,15},{1,0},{2,1},{3,2},{4,3},{5,4},{6,5},{7,6},{8,7},{9,8},{10,9... | collective-permute-start | bytes 41480 | tf_op jit(solution)/shard_map/ppermute | solution.py:232
  57.1 5.9 %collective-permute-start.4 = (f32[8,432]{1,0:T(8,128)S(1)}, f32[8,432]{1,0:T(8,128)S(1)}, u32[]{:S(2)}, u32[]{:S(2)}) collective-permute-start(f32[8,432]{1,0:T(8,128)S(1)} %collective-permute-done.3), channel_id=1, source_target_pairs={{0,1},{1,2},{2,3},{3,4},{4,5},{5,6},{6,7},{7,8},{8,9},{9,10},{10,1... | collective-permute-start | bytes 41480 | tf_op jit(solution)/shard_map/ppermute | solution.py:230
  57.9 5.9 %collective-permute-start.11 = (f32[8,432]{1,0:T(8,128)S(1)}, f32[8,432]{1,0:T(8,128)S(1)}, u32[]{:S(2)}, u32[]{:S(2)}) collective-permute-start(f32[8,432]{1,0:T(8,128)S(1)} %collective-permute-done.10), channel_id=1, source_target_pairs={{0,15},{1,0},{2,1},{3,2},{4,3},{5,4},{6,5},{7,6},{8,7},{9,8},{10,9... | collective-permute-start | bytes 41480 | tf_op jit(solution)/shard_map/ppermute | solution.py:232
  63.0 5.9 %collective-permute-start.5 = (f32[8,432]{1,0:T(8,128)S(1)}, f32[8,432]{1,0:T(8,128)S(1)}, u32[]{:S(2)}, u32[]{:S(2)}) collective-permute-start(f32[8,432]{1,0:T(8,128)S(1)} %collective-permute-done.4), channel_id=1, source_target_pairs={{0,1},{1,2},{2,3},{3,4},{4,5},{5,6},{6,7},{7,8},{8,9},{9,10},{10,1... | collective-permute-start | bytes 41480 | tf_op jit(solution)/shard_map/ppermute | solution.py:230
  63.8 5.9 %collective-permute-start.12 = (f32[8,432]{1,0:T(8,128)S(1)}, f32[8,432]{1,0:T(8,128)S(1)}, u32[]{:S(2)}, u32[]{:S(2)}) collective-permute-start(f32[8,432]{1,0:T(8,128)S(1)} %collective-permute-done.11), channel_id=1, source_target_pairs={{0,15},{1,0},{2,1},{3,2},{4,3},{5,4},{6,5},{7,6},{8,7},{9,8},{10,9... | collective-permute-start | bytes 41480 | tf_op jit(solution)/shard_map/ppermute | solution.py:232
  68.8 5.9 %collective-permute-start.6 = (f32[8,432]{1,0:T(8,128)S(1)}, f32[8,432]{1,0:T(8,128)S(1)}, u32[]{:S(2)}, u32[]{:S(2)}) collective-permute-start(f32[8,432]{1,0:T(8,128)S(1)} %collective-permute-done.5), channel_id=1, source_target_pairs={{0,1},{1,2},{2,3},{3,4},{4,5},{5,6},{6,7},{7,8},{8,9},{9,10},{10,1... | collective-permute-start | bytes 41480 | tf_op jit(solution)/shard_map/ppermute | solution.py:230
  69.1 28.2 %copy-start.35 = (f32[12]{0:T(128)S(1)}, f32[12]{0:T(128)}, u32[]{:S(2)}) copy-start(f32[12]{0:T(128)} %broadcast_multiply_fusion.5) | copy-start | bytes 148
  69.7 24.7 %collective-permute-start.13 = (f32[8,432]{1,0:T(8,128)S(1)}, f32[8,432]{1,0:T(8,128)S(1)}, u32[]{:S(2)}, u32[]{:S(2)}) collective-permute-start(f32[8,432]{1,0:T(8,128)S(1)} %collective-permute-done.12), channel_id=1, source_target_pairs={{0,15},{1,0},{2,1},{3,2},{4,3},{5,4},{6,5},{7,6},{8,7},{9,8},{10,9... | collective-permute-start | bytes 41480 | tf_op jit(solution)/shard_map/ppermute | solution.py:232
  74.7 20.9 %collective-permute-start.7 = (f32[8,432]{1,0:T(8,128)S(1)}, f32[8,432]{1,0:T(8,128)S(1)}, u32[]{:S(2)}, u32[]{:S(2)}) collective-permute-start(f32[8,432]{1,0:T(8,128)S(1)} %collective-permute-done.6), channel_id=1, source_target_pairs={{0,1},{1,2},{2,3},{3,4},{4,5},{5,6},{6,7},{7,8},{8,9},{9,10},{10,1... | collective-permute-start | bytes 41480 | tf_op jit(solution)/shard_map/ppermute | solution.py:230
  94.4 2.7 %collective-permute-start.14 = (f32[8,432]{1,0:T(8,128)S(1)}, f32[8,432]{1,0:T(8,128)S(1)}, u32[]{:S(2)}, u32[]{:S(2)}) collective-permute-start(f32[8,432]{1,0:T(8,128)S(1)} %collective-permute-done.13), channel_id=1, source_target_pairs={{0,15},{1,0},{2,1},{3,2},{4,3},{5,4},{6,5},{7,6},{8,7},{9,8},{10,9... | collective-permute-start | bytes 41480 | tf_op jit(solution)/shard_map/ppermute | solution.py:232
  97.3 4.2 %copy-start.25 = (f32[8,3]{0,1:T(4,128)S(1)}, f32[8,3]{0,1:T(4,128)}, u32[]{:S(2)}) copy-start(f32[8,3]{0,1:T(4,128)} %copy-done.24) | copy-start | bytes 292
  97.3 4.3 %copy-start.14 = (f32[8,3,3]{1,2,0:T(4,128)S(1)}, f32[8,3,3]{1,2,0:T(4,128)}, u32[]{:S(2)}) copy-start(f32[8,3,3]{1,2,0:T(4,128)} %copy.80) | copy-start | bytes 868
  97.3 4.8 %copy-start.18 = (f32[8,384]{1,0:T(8,128)S(1)}, f32[8,384]{1,0:T(8,128)}, u32[]{:S(2)}) copy-start(f32[8,384]{1,0:T(8,128)} %param.28) | copy-start | bytes 36868
  99.9 4.9 %copy-start.3 = (bf16[384,576]{0,1:T(8,128)(2,1)S(1)}, bf16[384,576]{0,1:T(8,128)(2,1)}, u32[]{:S(2)}) copy-start(bf16[384,576]{0,1:T(8,128)(2,1)} %param.42) | copy-start | bytes 1327108
  100.3 4.9 %copy-start.11 = (f32[8,3,3]{2,1,0:T(4,128)S(1)}, f32[8,3,3]{2,1,0:T(4,128)}, u32[]{:S(2)}) copy-start(f32[8,3,3]{2,1,0:T(4,128)} %copy-done.10) | copy-start | bytes 868
  100.4 5.2 %copy-start.13 = (f32[8,3,3]{0,2,1:T(4,128)S(1)}, f32[8,3,3]{0,2,1:T(4,128)}, u32[]{:S(2)}) copy-start(f32[8,3,3]{0,2,1:T(4,128)} %copy-done.12) | copy-start | bytes 868
  102.2 10.7 %copy-start.7 = (bf16[384,128]{1,0:T(8,128)(2,1)S(1)}, bf16[384,128]{1,0:T(8,128)(2,1)}, u32[]{:S(2)}) copy-start(bf16[384,128]{1,0:T(8,128)(2,1)} %param.34) | copy-start | bytes 294916
  102.6 35.6 %copy-start.16 = (f32[128]{0:T(128)S(1)}, f32[128]{0:T(128)}, u32[]{:S(2)}) copy-start(f32[128]{0:T(128)} %param.37) | copy-start | bytes 1540
  107.0 5.9 %collective-permute-start.15 = (f32[8,432]{1,0:T(8,128)S(1)}, f32[8,432]{1,0:T(8,128)S(1)}, u32[]{:S(2)}, u32[]{:S(2)}) collective-permute-start(f32[8,432]{1,0:T(8,128)S(1)} %reshape.281), channel_id=1, source_target_pairs={{0,1},{1,2},{2,3},{3,4},{4,5},{5,6},{6,7},{7,8},{8,9},{9,10},{10,1... | collective-permute-start | bytes 41480 | tf_op jit(solution)/shard_map/ppermute | solution.py:230
  107.7 29.2 %collective-permute-start.23 = (f32[8,432]{1,0:T(8,128)S(1)}, f32[8,432]{1,0:T(8,128)S(1)}, u32[]{:S(2)}, u32[]{:S(2)}) collective-permute-start(f32[8,432]{1,0:T(8,128)S(1)} %reshape.281), channel_id=1, source_target_pairs={{0,15},{1,0},{2,1},{3,2},{4,3},{5,4},{6,5},{7,6},{8,7},{9,8},{10,9... | collective-permute-start | bytes 41480 | tf_op jit(solution)/shard_map/ppermute | solution.py:232
  112.9 5.9 %copy-start.28 = (f32[8,432]{1,0:T(8,128)}, f32[8,432]{1,0:T(8,128)S(1)}, u32[]{:S(2)}) copy-start(f32[8,432]{1,0:T(8,128)S(1)} %collective-permute-done.15) | copy-start | bytes 41476
  112.9 5.9 %collective-permute-start.16 = (f32[8,432]{1,0:T(8,128)S(1)}, f32[8,432]{1,0:T(8,128)S(1)}, u32[]{:S(2)}, u32[]{:S(2)}) collective-permute-start(f32[8,432]{1,0:T(8,128)S(1)} %collective-permute-done.15), channel_id=1, source_target_pairs={{0,1},{1,2},{2,3},{3,4},{4,5},{5,6},{6,7},{7,8},{8,9},{9,10},{10,1... | collective-permute-start | bytes 41480 | tf_op jit(solution)/shard_map/ppermute | solution.py:230
  118.7 19.4 %collective-permute-start.17 = (f32[8,432]{1,0:T(8,128)S(1)}, f32[8,432]{1,0:T(8,128)S(1)}, u32[]{:S(2)}, u32[]{:S(2)}) collective-permute-start(f32[8,432]{1,0:T(8,128)S(1)} %collective-permute-done.16), channel_id=1, source_target_pairs={{0,1},{1,2},{2,3},{3,4},{4,5},{5,6},{6,7},{7,8},{8,9},{9,10},{10,1... | collective-permute-start | bytes 41480 | tf_op jit(solution)/shard_map/ppermute | solution.py:230
  136.9 29.6 %collective-permute-start.24 = (f32[8,432]{1,0:T(8,128)S(1)}, f32[8,432]{1,0:T(8,128)S(1)}, u32[]{:S(2)}, u32[]{:S(2)}) collective-permute-start(f32[8,432]{1,0:T(8,128)S(1)} %collective-permute-done.23), channel_id=1, source_target_pairs={{0,15},{1,0},{2,1},{3,2},{4,3},{5,4},{6,5},{7,6},{8,7},{9,8},{10,9... | collective-permute-start | bytes 41480 | tf_op jit(solution)/shard_map/ppermute | solution.py:232
  138.2 32.9 %collective-permute-start.18 = (f32[8,432]{1,0:T(8,128)S(1)}, f32[8,432]{1,0:T(8,128)S(1)}, u32[]{:S(2)}, u32[]{:S(2)}) collective-permute-start(f32[8,432]{1,0:T(8,128)S(1)} %collective-permute-done.17), channel_id=1, source_target_pairs={{0,1},{1,2},{2,3},{3,4},{4,5},{5,6},{6,7},{7,8},{8,9},{9,10},{10,1... | collective-permute-start | bytes 41480 | tf_op jit(solution)/shard_map/ppermute | solution.py:230
  138.2 38.7 %copy-start.31 = (bf16[128,12]{0,1:T(8,128)(2,1)S(1)}, bf16[128,12]{0,1:T(8,128)(2,1)}, u32[]{:S(2)}) copy-start(bf16[128,12]{0,1:T(8,128)(2,1)} %param.43) | copy-start | bytes 9220
  166.6 42.7 %copy-start.29 = (f32[8,432]{1,0:T(8,128)S(1)}, f32[8,432]{1,0:T(8,128)}, u32[]{:S(2)}) copy-start(f32[8,432]{1,0:T(8,128)} %copy-done.28) | copy-start | bytes 41476
  166.6 42.7 %copy-start.27 = (f32[8,432]{1,0:T(8,128)S(1)}, f32[8,432]{1,0:T(8,128)}, u32[]{:S(2)}) copy-start(f32[8,432]{1,0:T(8,128)} %copy-done.26) | copy-start | bytes 41476
  166.6 5.9 %collective-permute-start.25 = (f32[8,432]{1,0:T(8,128)S(1)}, f32[8,432]{1,0:T(8,128)S(1)}, u32[]{:S(2)}, u32[]{:S(2)}) collective-permute-start(f32[8,432]{1,0:T(8,128)S(1)} %collective-permute-done.24), channel_id=1, source_target_pairs={{0,15},{1,0},{2,1},{3,2},{4,3},{5,4},{6,5},{7,6},{8,7},{9,8},{10,9... | collective-permute-start | bytes 41480 | tf_op jit(solution)/shard_map/ppermute | solution.py:232
  171.1 5.9 %collective-permute-start.19 = (f32[8,432]{1,0:T(8,128)S(1)}, f32[8,432]{1,0:T(8,128)S(1)}, u32[]{:S(2)}, u32[]{:S(2)}) collective-permute-start(f32[8,432]{1,0:T(8,128)S(1)} %collective-permute-done.18), channel_id=1, source_target_pairs={{0,1},{1,2},{2,3},{3,4},{4,5},{5,6},{6,7},{7,8},{8,9},{9,10},{10,1... | collective-permute-start | bytes 41480 | tf_op jit(solution)/shard_map/ppermute | solution.py:230
  172.5 5.9 %collective-permute-start.26 = (f32[8,432]{1,0:T(8,128)S(1)}, f32[8,432]{1,0:T(8,128)S(1)}, u32[]{:S(2)}, u32[]{:S(2)}) collective-permute-start(f32[8,432]{1,0:T(8,128)S(1)} %collective-permute-done.25), channel_id=1, source_target_pairs={{0,15},{1,0},{2,1},{3,2},{4,3},{5,4},{6,5},{7,6},{8,7},{9,8},{10,9... | collective-permute-start | bytes 41480 | tf_op jit(solution)/shard_map/ppermute | solution.py:232
  176.9 5.9 %collective-permute-start.20 = (f32[8,432]{1,0:T(8,128)S(1)}, f32[8,432]{1,0:T(8,128)S(1)}, u32[]{:S(2)}, u32[]{:S(2)}) collective-permute-start(f32[8,432]{1,0:T(8,128)S(1)} %collective-permute-done.19), channel_id=1, source_target_pairs={{0,1},{1,2},{2,3},{3,4},{4,5},{5,6},{6,7},{7,8},{8,9},{9,10},{10,1... | collective-permute-start | bytes 41480 | tf_op jit(solution)/shard_map/ppermute | solution.py:230
  178.4 5.9 %collective-permute-start.27 = (f32[8,432]{1,0:T(8,128)S(1)}, f32[8,432]{1,0:T(8,128)S(1)}, u32[]{:S(2)}, u32[]{:S(2)}) collective-permute-start(f32[8,432]{1,0:T(8,128)S(1)} %collective-permute-done.26), channel_id=1, source_target_pairs={{0,15},{1,0},{2,1},{3,2},{4,3},{5,4},{6,5},{7,6},{8,7},{9,8},{10,9... | collective-permute-start | bytes 41480 | tf_op jit(solution)/shard_map/ppermute | solution.py:232
  182.8 5.9 %collective-permute-start.21 = (f32[8,432]{1,0:T(8,128)S(1)}, f32[8,432]{1,0:T(8,128)S(1)}, u32[]{:S(2)}, u32[]{:S(2)}) collective-permute-start(f32[8,432]{1,0:T(8,128)S(1)} %collective-permute-done.20), channel_id=1, source_target_pairs={{0,1},{1,2},{2,3},{3,4},{4,5},{5,6},{6,7},{7,8},{8,9},{9,10},{10,1... | collective-permute-start | bytes 41480 | tf_op jit(solution)/shard_map/ppermute | solution.py:230
  183.0 27.9 %copy-start.36 = (f32[12]{0:T(128)S(1)}, f32[12]{0:T(128)}, u32[]{:S(2)}) copy-start(f32[12]{0:T(128)} %broadcast_multiply_fusion.5) | copy-start | bytes 148
  184.2 23.6 %collective-permute-start.28 = (f32[8,432]{1,0:T(8,128)S(1)}, f32[8,432]{1,0:T(8,128)S(1)}, u32[]{:S(2)}, u32[]{:S(2)}) collective-permute-start(f32[8,432]{1,0:T(8,128)S(1)} %collective-permute-done.27), channel_id=1, source_target_pairs={{0,15},{1,0},{2,1},{3,2},{4,3},{5,4},{6,5},{7,6},{8,7},{9,8},{10,9... | collective-permute-start | bytes 41480 | tf_op jit(solution)/shard_map/ppermute | solution.py:232
  188.7 20.5 %collective-permute-start.22 = (f32[8,432]{1,0:T(8,128)S(1)}, f32[8,432]{1,0:T(8,128)S(1)}, u32[]{:S(2)}, u32[]{:S(2)}) collective-permute-start(f32[8,432]{1,0:T(8,128)S(1)} %collective-permute-done.21), channel_id=1, source_target_pairs={{0,1},{1,2},{2,3},{3,4},{4,5},{5,6},{6,7},{7,8},{8,9},{9,10},{10,1... | collective-permute-start | bytes 41480 | tf_op jit(solution)/shard_map/ppermute | solution.py:230
  206.9 4.3 %copy-start.44 = (pred[128]{0:T(512)(128)(4,1)S(1)}, pred[128]{0:T(512)(128)(4,1)}, u32[]{:S(2)}) copy-start(pred[128]{0:T(512)(128)(4,1)} %broadcast_compare_fusion.1) | copy-start | bytes 388
  207.9 2.7 %collective-permute-start.29 = (f32[8,432]{1,0:T(8,128)S(1)}, f32[8,432]{1,0:T(8,128)S(1)}, u32[]{:S(2)}, u32[]{:S(2)}) collective-permute-start(f32[8,432]{1,0:T(8,128)S(1)} %collective-permute-done.28), channel_id=1, source_target_pairs={{0,15},{1,0},{2,1},{3,2},{4,3},{5,4},{6,5},{7,6},{8,7},{9,8},{10,9... | collective-permute-start | bytes 41480 | tf_op jit(solution)/shard_map/ppermute | solution.py:232
  (11 other events, 22.0 us)
